TPU v7x, 256 devices: a whole 4x4x8 slice. The times are simulated.
256 devices in a mesh: seq: 16 (over x, y_lo, core), ch: 16 (over z, y_hi).
Axes of the slice: x: 4, y: 4 (y_hi: 2, y_lo: 2; y = y_hi * 2 + y_lo), z: 8, core: 2. Of those that a mesh axis runs over, the one named last changes fastest.
Arguments:
- grad_out: bfloat16 [2048, 8192], P('seq', 'ch'), may hold values from -6 to 6
- out_weight: bfloat16 [8192, 8192], P('ch'), may hold values from -0.0625 to 0.0625
- query_gate: bfloat16 [2048, 8192], P('seq', 'ch'), may hold values from -6 to 6
- key_branch: bfloat16 [2048, 8192], P('seq', 'ch'), may hold values from -6 to 6
- value_branch: bfloat16 [2048, 8192], P('seq', 'ch'), may hold values from -6 to 6
- filter_taps: bfloat16 [2048, 8192], P('seq', 'ch'), may hold values from -4 to 4
Outputs:
- key_grad: bfloat16 [2048, 8192], P('seq', 'ch')
- value_grad: bfloat16 [2048, 8192], P('seq', 'ch')
- filter_grad: float32 [2048, 8192], P('seq', 'ch')
All inputs are finite; a program needn't handle non-finite values.
Results may differ from a plain program's by a relative error of at most 0.017.
Values may be sent and summed in bfloat16 or wider, within the bound.
A program may use at most 192 MiB of HBM per device.

v0:
```python
import math
import jax
import jax.numpy as jnp
from jax import lax
from jax.sharding import PartitionSpec as P


def build_tables(seg_len):
    twice_length = 2 * seg_len
    freq_index = jnp.arange(twice_length, dtype=jnp.int32)
    row_index = jnp.arange(seg_len, dtype=jnp.int32)
    angle_unit = 2.0 * math.pi / twice_length
    fwd_phase = (freq_index[:, None] * row_index[None, :] % twice_length).astype(
        jnp.float32
    ) * angle_unit
    back_phase = (freq_index[None, :] * (seg_len - row_index[:, None]) % twice_length).astype(
        jnp.float32
    ) * angle_unit
    window_pos = (freq_index + seg_len) % twice_length
    window_phase = (freq_index[None, :] * window_pos[:, None] % twice_length).astype(
        jnp.float32
    ) * angle_unit
    parity = jnp.where(freq_index % 2 == 0, 1.0, -1.0).astype(jnp.float32)[:, None]
    return (
        jnp.cos(fwd_phase).astype(jnp.bfloat16),
        jnp.sin(fwd_phase).astype(jnp.bfloat16),
        jnp.cos(back_phase).astype(jnp.bfloat16),
        jnp.sin(back_phase).astype(jnp.bfloat16),
        jnp.cos(window_phase).astype(jnp.bfloat16),
        jnp.sin(window_phase).astype(jnp.bfloat16),
        parity,
    )


def spectra(block_list, cosine_forward, sine_forward):
    cosine_piece = jnp.einsum(
        "qk,rkb->rqb", cosine_forward, block_list, preferred_element_type=jnp.float32
    )
    sine_piece = jnp.einsum(
        "qk,rkb->rqb", sine_forward, block_list, preferred_element_type=jnp.float32
    )
    return (cosine_piece, sine_piece)


def shards(grad_out, out_weight, query_gate, key_branch, value_branch, filter_taps):
    seg_len = query_gate.shape[0]
    channels = query_gate.shape[1]
    twice_length = 2 * seg_len
    segments = lax.axis_size("seq")
    my_index = lax.axis_index("seq")
    factor = 1.0 / math.sqrt(seg_len * segments)
    grad_mix = lax.dot_general(
        lax.all_gather(grad_out, "ch", axis=1, tiled=True),
        out_weight,
        (((1,), (1,)), ((), ())),
        preferred_element_type=jnp.float32,
    )
    gated_grad = (grad_mix * query_gate.astype(jnp.float32)).astype(jnp.bfloat16)
    conv_input = (key_branch.astype(jnp.float32) * value_branch.astype(jnp.float32)).astype(
        jnp.bfloat16
    )
    tables = build_tables(seg_len)
    (
        cosine_forward,
        sine_forward,
        cosine_backward,
        sine_backward,
        cosine_window,
        sine_window,
        parity,
    ) = tables
    all_taps = lax.all_gather(filter_taps, "seq", axis=0, tiled=True)
    tap_cos, tap_sin = spectra(
        all_taps.reshape(segments, seg_len, channels), cosine_forward, sine_forward
    )
    kern_cos = jnp.concatenate([jnp.zeros_like(tap_cos[:1]), tap_cos[:-1]], 0) + parity * tap_cos
    kern_sin = jnp.concatenate([jnp.zeros_like(tap_sin[:1]), tap_sin[:-1]], 0) + parity * tap_sin
    own_cos, own_sin = spectra(conv_input[None], cosine_forward, sine_forward)
    own_cos = own_cos[0]
    own_sin = own_sin[0]
    zero_spec = jnp.zeros((twice_length, channels), jnp.float32)
    initial = (zero_spec, zero_spec, jnp.zeros(((segments + 1) * seg_len, channels), jnp.float32))
    piece_data = lax.all_gather(gated_grad, "seq", axis=0, tiled=True)
    block_count = piece_data.shape[0] // seg_len
    seg_ids = jnp.arange(block_count, dtype=jnp.int32)
    block_list = piece_data.reshape(block_count, seg_len, channels)
    grad_cos, grad_sin = spectra(block_list, cosine_forward, sine_forward)
    lag_steps = seg_ids - my_index
    inside = seg_ids < segments
    live_mask = ((lag_steps >= 0) & inside).astype(jnp.float32)[:, None, None]
    lag_clip = jnp.clip(lag_steps, 0, segments - 1)
    lag_kcos = jnp.take(kern_cos, lag_clip, axis=0)
    lag_ksin = jnp.take(kern_sin, lag_clip, axis=0)
    running_real = jnp.sum(live_mask * (grad_cos * lag_kcos + grad_sin * lag_ksin), axis=0)
    running_imaginary = jnp.sum(live_mask * (grad_sin * lag_kcos - grad_cos * lag_ksin), axis=0)
    product_real = (own_cos * grad_cos + own_sin * grad_sin).astype(jnp.bfloat16)
    product_imaginary = (own_sin * grad_cos - own_cos * grad_sin).astype(jnp.bfloat16)
    windows = jnp.einsum(
        "an,hny->hay", cosine_window, product_real, preferred_element_type=jnp.float32
    ) - jnp.einsum(
        "an,hny->hay", sine_window, product_imaginary, preferred_element_type=jnp.float32
    )
    windows = windows * (live_mask / twice_length)

    def place(item_index, buffer):
        offset = lag_clip[item_index] * seg_len
        current = lax.dynamic_slice_in_dim(buffer, offset, twice_length, 0)
        return lax.dynamic_update_slice_in_dim(buffer, current + windows[item_index], offset, 0)

    buffer = lax.fori_loop(0, block_list.shape[0], place, initial[2])
    convolution_gradient = (
        jnp.dot(
            cosine_backward, running_real.astype(jnp.bfloat16), preferred_element_type=jnp.float32
        )
        - jnp.dot(
            sine_backward,
            running_imaginary.astype(jnp.bfloat16),
            preferred_element_type=jnp.float32,
        )
    ) / twice_length
    own_rows = lax.psum_scatter(
        buffer[seg_len:].astype(jnp.bfloat16), "seq", scatter_dimension=0, tiled=True
    ).astype(jnp.float32)
    filter_grad = own_rows * factor
    key_grad = (convolution_gradient * value_branch.astype(jnp.float32)).astype(jnp.bfloat16)
    value_grad = (convolution_gradient * key_branch.astype(jnp.float32)).astype(jnp.bfloat16)
    return (key_grad, value_grad, filter_grad)


def solution(mesh):
    return jax.shard_map(
        shards,
        mesh=mesh,
        in_specs=(
            P("seq", "ch"),
            P("ch", None),
            P("seq", "ch"),
            P("seq", "ch"),
            P("seq", "ch"),
            P("seq", "ch"),
        ),
        out_specs=(P("seq", "ch"), P("seq", "ch"), P("seq", "ch")),
        check_vma=False,
    )
```

profile of v0, /device:TPU:32, one launch (start us, length us, event | category | flops | bytes accessed | tf_op | source)
XLA Modules:
  0.0 391.5 jit_solution(9335437715561925159)
XLA Ops:
  7.2 0.7 all-gather.4.cloned.1.call-update
  8.0 0.7 all-gather.8.cloned.1.call-update
  8.7 88.9 %all-gather.4.cloned.1.call-done = bf16[128,8192]{1,0:T(8,128)(2,1)} async-done(((bf16[128,512]{1,0:T(8,128)(2,1)}), bf16[128,8192]{1,0:T(8,128)(2,1)}) %all-gather.4.cloned.1.call-update) | async-done | bytes 2097168 | tf_op jit(solution)/shard_map/all_gather | solution.py:53
  97.6 7.6 %fusion.22 = bf16[128,512]{1,0:T(8,128)(2,1)} fusion(bf16[128,8192]{1,0:T(8,128)(2,1)} %all-gather.4.cloned.1.call-done, bf16[512,8192]{1,0:T(8,128)(2,1)} %param.11, bf16[128,512]{1,0:T(8,128)(2,1)} %param.12), kind=kOutput, calls=%fused_computation.40 | convolution fusion | flops 1073938432 | bytes 10747904 | tf_op jit(solution)/shard_map/dot_general | solution.py:52
  105.4 0.7 convolution_bitcast_fusion.2
  106.1 0.7 convolution_bitcast_fusion.3
  106.8 25.7 %all-gather.8.cloned.1.call-done = bf16[2048,512]{1,0:T(8,128)(2,1)} async-done(((bf16[128,512]{1,0:T(8,128)(2,1)}), bf16[2048,512]{1,0:T(8,128)(2,1)}) %all-gather.8.cloned.1.call-update) | async-done | bytes 2097168 | tf_op jit(solution)/shard_map/all_gather | solution.py:72
  132.5 3.2 convolution_bitcast_fusion.1
  135.7 4.5 %slice.17 = f32[15,256,512]{2,1,0:T(8,128)} slice(f32[16,256,512]{2,1,0:T(8,128)S(1)} %convolution_bitcast_fusion.1), slice={[0:15], [0:256], [0:512]} | slice | bytes 15728640 | tf_op jit(solution)/shard_map/slice | solution.py:76
  140.3 1.7 convolution_bitcast_fusion
  142.0 3.2 copy-done.1
  145.2 4.6 %slice.18 = f32[15,256,512]{2,1,0:T(8,128)} slice(f32[16,256,512]{2,1,0:T(8,128)S(1)} %convolution_bitcast_fusion), slice={[0:15], [0:256], [0:512]} | slice | bytes 15728640 | tf_op jit(solution)/shard_map/slice | solution.py:77
  149.8 18.9 %multiply_add_fusion.1 = (f32[16,256,512]{2,1,0:T(8,128)}, f32[16,256,512]{2,1,0:T(8,128)}) fusion(f32[16,256,512]{2,1,0:T(8,128)} %copy-done, f32[15,256,512]{2,1,0:T(8,128)} %slice.17, f32[256]{0:T(256)S(1)} %compare_select_fusion.3, f32[16,256,512]{2,1,0:T(8,128)} %copy-done.1, f32[15,256,512]{2,1,0:T(8,128)} %slice.18), kind=kLoop, calls=%fused_computation.25 | loop fusion | flops 8388608 | bytes 49284096 | tf_op jit(solution)/shard_map/add | solution.py:76
  168.7 7.7 %gather_fusion = f32[16,256,512]{2,1,0:T(8,128)} fusion(f32[16,256,512]{2,1,0:T(8,128)} %get-tuple-element.108, s32[1024]{0:T(1024)S(1)} %pad_clamp_fusion), kind=kCustom, calls=%fused_computation.clone | custom fusion | bytes 16777280 | tf_op jit(solution)/shard_map/jit(_take)/gather | solution.py:92
  176.4 9.2 %copy.18 = f32[16,256,512]{1,2,0:T(8,128)} copy(f32[16,256,512]{2,1,0:T(8,128)} %gather_fusion) | data formatting | bytes 16777216 | tf_op jit(solution)/shard_map/jit(_take)/gather | solution.py:92
  185.7 7.7 %gather_fusion.1 = f32[16,256,512]{2,1,0:T(8,128)} fusion(f32[16,256,512]{2,1,0:T(8,128)} %get-tuple-element.109, s32[1024]{0:T(1024)S(1)} %pad_clamp_fusion), kind=kCustom, calls=%fused_computation.1.clone | custom fusion | bytes 16777280 | tf_op jit(solution)/shard_map/jit(_take)/gather | solution.py:93
  193.3 9.3 %copy.20 = f32[16,256,512]{1,2,0:T(8,128)} copy(f32[16,256,512]{2,1,0:T(8,128)} %gather_fusion.1) | data formatting | bytes 16777216 | tf_op jit(solution)/shard_map/jit(_take)/gather | solution.py:93
  202.6 3.5 fusion.57
  206.1 10.9 %fusion.6 = (bf16[256,512]{0,1:T(8,128)(2,1)S(1)}, bf16[256,512]{0,1:T(8,128)(2,1)S(1)}, f32[16,512,256]{2,1,0:T(8,128)}) fusion(f32[16,512,256]{2,1,0:T(8,128)S(1)} %fusion.57, f32[16,256,512]{1,2,0:T(8,128)} %copy.20, f32[16,256,512]{1,2,0:T(8,128)} %copy.18, f32[16]{0:T(128)S(1)} %get-tuple-element.114, pred[16]{0:T(512)(128)(4,1)S(1)} %get-tuple-element.113, ...), kind=kOutput, calls=%fused_computation.14 | convolution fusion | flops 562266112 | bytes 36175952 | tf_op jit(solution)/shard_map/qk,rkb->rqb/dot_general | solution.py:39
  217.0 9.5 %fusion.11 = f32[16,512,256]{2,1,0:T(8,128)} fusion(f32[16,512,256]{2,1,0:T(8,128)} %get-tuple-element.110, f32[16,512,256]{2,1,0:T(8,128)S(1)} %fusion.57, f32[256,512]{0,1:T(8,128)S(1)} %convolution_bitcast_fusion.2, f32[256,512]{0,1:T(8,128)S(1)} %convolution_bitcast_fusion.3, s32[256]{0:T(256)S(1)} %and_select_fusion), kind=kOutput, calls=%fused_computation.26 | convolution fusion | flops 1083113472 | bytes 26215424 | tf_op jit(solution)/shard_map/an,hny->hay/dot_general | solution.py:100
  226.4 11.8 %multiply_bitcast_fusion = f32[16,256,512]{1,2,0:T(8,128)} fusion(f32[16,512,256]{2,1,0:T(8,128)} %fusion.11, f32[16]{0:T(128)S(1)} %broadcast_select_fusion, f32[16,512,256]{2,1,0:T(8,128)} %get-tuple-element.110, f32[16,512,256]{2,1,0:T(8,128)S(1)} %fusion.57, f32[256,512]{0,1:T(8,128)S(1)} %convolution_bitcast_fusion.2, ...), kind=kOutput, calls=%fused_computation.23 | convolution fusion | flops 1087307776 | bytes 34604096 | tf_op jit(solution)/shard_map/an,hny->hay/dot_general | solution.py:98
  238.3 2.6 broadcast_in_dim.30
  240.9 71.4 %while.13 = (s32[]{:T(128)}, f32[2176,512]{1,0:T(8,128)}, s32[16]{0:T(128)S(1)}, f32[16,256,512]{1,2,0:T(8,128)}, s32[]{:T(128)}, /*index=5*/s32[1]{0:T(128)}, s32[]{:T(128)}, s32[]{:T(128)}) while((s32[]{:T(128)}, f32[2176,512]{1,0:T(8,128)}, s32[16]{0:T(128)S(1)}, f32[16,256,512]{1,2,0:T(8,128)}, s32[]{:T(128)}, /*index=5*/s32[1]{0:T(128)}, ...), condition=%wide.region_3.5_spmd, body=%wide.region_2.4_spmd.sunk | while | flops 131078 | bytes 3670167 | solution.py:110
  242.1 1.1 constant_dynamic-slice_fusion.2
  243.4 1.9 fusion.115
  246.6 1.1 constant_dynamic-slice_fusion.2
  247.9 1.9 fusion.115
  251.0 1.1 constant_dynamic-slice_fusion.2
  252.3 1.9 fusion.115
  255.5 1.1 constant_dynamic-slice_fusion.2
  256.8 1.9 fusion.115
  258.7 0.6 dynamic_slice.28
  260.0 1.1 constant_dynamic-slice_fusion.2
  261.2 2.0 fusion.115
  263.2 0.6 dynamic_slice.28
  264.4 1.1 constant_dynamic-slice_fusion.2
  265.7 1.9 fusion.115
  268.9 1.1 constant_dynamic-slice_fusion.2
  270.2 1.9 fusion.115
  273.4 1.1 constant_dynamic-slice_fusion.2
  274.7 1.9 fusion.115
  276.6 0.6 dynamic_slice.28
  277.8 1.1 constant_dynamic-slice_fusion.2
  279.1 1.9 fusion.115
  281.1 0.6 dynamic_slice.28
  282.3 1.1 constant_dynamic-slice_fusion.2
  283.6 1.9 fusion.115
  286.8 1.1 constant_dynamic-slice_fusion.2
  288.1 1.9 fusion.115
  291.2 1.1 constant_dynamic-slice_fusion.2
  292.5 1.9 fusion.115
  295.7 1.1 constant_dynamic-slice_fusion.2
  297.0 1.9 fusion.115
  300.1 1.1 constant_dynamic-slice_fusion.2
  301.4 1.9 fusion.115
  304.6 1.1 constant_dynamic-slice_fusion.2
  305.9 1.9 fusion.115
  309.1 1.1 constant_dynamic-slice_fusion.2
  310.3 1.9 fusion.115
  312.3 3.8 slice.21
  316.1 0.7 fusion.32
  316.8 1.4 fusion.24
  318.2 65.2 %reduce-scatter.2.cloned.1.call-done = bf16[128,512]{1,0:T(8,128)(2,1)} async-done(((bf16[2048,512]{1,0:T(8,128)(2,1)}), bf16[128,512]{1,0:T(8,128)(2,1)}) %reduce-scatter.2.cloned.1.call-update) | async-done | bytes 131088 | tf_op jit(solution)/shard_map/reduce_scatter | solution.py:121
  383.4 1.6 convert_multiply_fusion.3
  (53 shorter events, 10.4 us)
Async XLA Ops:
  7.2 98.2 %copy-start.4 = (bf16[128,512]{1,0:T(8,128)(2,1)S(1)}, bf16[128,512]{1,0:T(8,128)(2,1)}, u32[]{:S(2)}) copy-start(bf16[128,512]{1,0:T(8,128)(2,1)} %param.13) | copy-start | bytes 393220
  7.2 98.2 %copy-start.5 = (bf16[128,512]{1,0:T(8,128)(2,1)S(1)}, bf16[128,512]{1,0:T(8,128)(2,1)}, u32[]{:S(2)}) copy-start(bf16[128,512]{1,0:T(8,128)(2,1)} %param.14) | copy-start | bytes 393220
  7.2 90.4 %all-gather.4.cloned.1.call-start = ((), (), s32[]{:S(2)}) async-start(), calls=%async_computation.1 | async-start | bytes 2228224 | tf_op jit(solution)/shard_map/all_gather | solution.py:53
  7.9 124.6 %all-gather.8.cloned.1.call-start = ((), (), s32[]{:S(2)}) async-start(), calls=%async_computation.3 | async-start | bytes 2228224 | tf_op jit(solution)/shard_map/all_gather | solution.py:72
  8.7 193.9 %all-gather.6.cloned.1.call-start = ((), (), s32[]{:S(2)}) async-start(), calls=%async_computation.2 | async-start | bytes 2228224 | tf_op jit(solution)/shard_map/all_gather | solution.py:83
  105.2 278.1 %reduce-scatter.2.cloned.1.call-start = ((), (), s32[]{:S(2)}) async-start(), calls=%async_computation.4 | async-start | bytes 2228224 | tf_op jit(solution)/shard_map/reduce_scatter | solution.py:121
  135.7 6.2 %copy-start = (f32[16,256,512]{2,1,0:T(8,128)}, f32[16,256,512]{2,1,0:T(8,128)S(1)}, u32[]{:S(2)}) copy-start(f32[16,256,512]{2,1,0:T(8,128)S(1)} %convolution_bitcast_fusion.1) | copy-start | bytes 25165828
  135.7 4.6 %copy-start.2 = (bf16[2048,512]{1,0:T(8,128)(2,1)S(1)}, bf16[2048,512]{1,0:T(8,128)(2,1)}, u32[]{:S(2)}) copy-start(bf16[2048,512]{1,0:T(8,128)(2,1)} %all-gather.8.cloned.1.call-done) | copy-start | bytes 6291460
  141.9 3.2 copy-start.1
  202.6 3.5 copy-start.3
Sparse Core Ops, SparseCore 0:
  10.5 87.1 all-gather.3
  99.5 32.9 all-gather.7
  134.9 36.3 all-gather.5
  316.2 67.0 reduce-scatter.1
where the time goes:
time: 394 us; the launch traced here: 392 us
  waiting for transfers between devices  181 us (46%)
  local copies, waits for them, and re-layouts  82.5 us (21%)
  matrix products  51.6 us (13%)
  other arithmetic  51.5 us (13%)
  between operations  13.9 us (4%)
  loops' own time  10.7 us (3%)
    all_gather x1, waiting for transfers between devices, shards(): lax.all_gather(grad_out, 'ch', axis=1, tiled=True)  88.9 us
    reduce_scatter x1, waiting for transfers between devices, shards(): lax.psum_scatter(buffer[seg_len:].astype(jnp.bfloat16), 'seq', scatter_di...  65.2 us
    dynamic_update_slice x16, other arithmetic, place(): lax.dynamic_update_slice_in_dim(buffer, current + windows[item_index], of...  30.9 us
    all_gather x1, waiting for transfers between devices, shards(): all_taps = lax.all_gather(filter_taps, 'seq', axis=0, tiled=True)  25.7 us
    dynamic_slice x32, local copies, waits for them, and re-layouts, place(): windows[item_index]  20.5 us
    add x1, other arithmetic, shards(): jnp.concatenate([jnp.zeros_like(tap_cos[:1]), tap_cos[:-1]], 0)  18.9 us
    gather x2, local copies, waits for them, and re-layouts, shards(): lag_kcos = jnp.take(kern_cos, lag_clip, axis=0)  17 us
    gather x2, local copies, waits for them, and re-layouts, shards(): lag_ksin = jnp.take(kern_sin, lag_clip, axis=0)  16.9 us
  transfers between devices with their start and end apart: 4, of which 3 were waited for; matrix products, arithmetic and copies ran while one was open for 20% of the time, Pallas kernels for 0%

commit v1 on v0

--- a/solution.py
+++ b/solution.py
@@ -69,7 +69,15 @@
         sine_window,
         parity,
     ) = tables
-    all_taps = lax.all_gather(filter_taps, "seq", axis=0, tiled=True)
+    all_taps = jnp.concatenate(
+        lax.all_to_all(
+            jnp.stack([filter_taps] * lax.axis_size("seq"), 0),
+            concat_axis=0,
+            split_axis=0,
+            axis_name="seq",
+        ),
+        0,
+    )
     tap_cos, tap_sin = spectra(
         all_taps.reshape(segments, seg_len, channels), cosine_forward, sine_forward
     )

time: 394 us -> 378 us (0.959)
  waiting for transfers between devices: 181 us -> 158 us
  starting transfers between devices: 0.16 us -> 5.54 us
    all_gather x1 -> x0, waiting for transfers between devices: 25.7 us -> none  [shards(): all_taps = lax.all_gather(filter_taps, 'seq', axis=0, tiled=True)]
    all_gather x1, waiting for transfers between devices: 88.9 us -> 95.8 us  [shards(): lax.all_gather(grad_out, 'ch', axis=1, tiled=True)]
    all_to_all x0 -> x1, starting transfers between devices: none -> 5.42 us  [shards(): lax.all_to_all(jnp.stack([filter_taps] * lax.axis_size('seq'), 0), concat...]
  transfers between devices with their start and end apart: 4 -> 4, of which waited for: 3 -> 2; matrix products, arithmetic and copies ran while one was open for 20% -> 21% of each run, Pallas kernels for 0% -> 0%
where the time goes in v1:
time: 378 us; the launch traced here: 375 us
  waiting for transfers between devices  158 us (42%)
  local copies, waits for them, and re-layouts  85.3 us (23%)
  other arithmetic  51.6 us (14%)
  matrix products  50 us (13%)
  between operations  13.9 us (4%)
  loops' own time  10.7 us (3%)
  starting transfers between devices  5.54 us (1%)
    all_gather x1, waiting for transfers between devices, shards(): lax.all_gather(grad_out, 'ch', axis=1, tiled=True)  95.8 us
    reduce_scatter x1, waiting for transfers between devices, shards(): lax.psum_scatter(buffer[seg_len:].astype(jnp.bfloat16), 'seq', scatter_di...  61.7 us
    dynamic_update_slice x16, other arithmetic, place(): lax.dynamic_update_slice_in_dim(buffer, current + windows[item_index], of...  30.9 us
    dynamic_slice x32, local copies, waits for them, and re-layouts, place(): windows[item_index]  20.5 us
    add x1, other arithmetic, shards(): jnp.concatenate([jnp.zeros_like(tap_cos[:1]), tap_cos[:-1]], 0)  19 us
    gather x2, local copies, waits for them, and re-layouts, shards(): lag_ksin = jnp.take(kern_sin, lag_clip, axis=0)  16.9 us
    gather x2, local copies, waits for them, and re-layouts, shards(): lag_kcos = jnp.take(kern_cos, lag_clip, axis=0)  16.9 us
    dot_general x3, matrix products, spectra(): jnp.einsum('qk,rkb->rqb', sine_forward, block_list, preferred_element_typ...  13.3 us
  transfers between devices with their start and end apart: 4, of which 2 were waited for; matrix products, arithmetic and copies ran while one was open for 21% of the time, Pallas kernels for 0%

profile of v1, /device:TPU:32, one launch (start us, length us, event | category | flops | bytes accessed | tf_op | source)
XLA Modules:
  0.0 375.3 jit_solution(4942925238591469975)
XLA Ops:
  7.2 0.7 all-gather.3.cloned.1.call-update
  7.9 2.5 stack.2
  10.4 5.4 %all-to-all-start = ((bf16[16,128,512]{2,1,0:T(8,128)(2,1)}), bf16[16,128,512]{2,1,0:T(8,128)(2,1)S(1)}, u32[]{:S(2)}, u32[]{:S(2)}) async-start(bf16[16,128,512]{2,1,0:T(8,128)(2,1)} %stack.2), calls=%async_computation | async-start | bytes 4194304 | tf_op jit(solution)/shard_map/all_to_all | solution.py:73
  15.9 95.8 %all-gather.3.cloned.1.call-done = bf16[128,8192]{1,0:T(8,128)(2,1)} async-done(((bf16[128,512]{1,0:T(8,128)(2,1)}), bf16[128,8192]{1,0:T(8,128)(2,1)}) %all-gather.3.cloned.1.call-update) | async-done | bytes 2097168 | tf_op jit(solution)/shard_map/all_gather | solution.py:53
  111.7 7.6 %fusion.22 = bf16[128,512]{1,0:T(8,128)(2,1)} fusion(bf16[128,8192]{1,0:T(8,128)(2,1)} %all-gather.3.cloned.1.call-done, bf16[512,8192]{1,0:T(8,128)(2,1)} %param.11, bf16[128,512]{1,0:T(8,128)(2,1)} %param.12), kind=kOutput, calls=%fused_computation.40 | convolution fusion | flops 1073938432 | bytes 10747904 | tf_op jit(solution)/shard_map/dot_general | solution.py:52
  119.5 0.7 convolution_bitcast_fusion.2
  120.2 0.7 convolution_bitcast_fusion.3
  120.9 1.7 convolution_bitcast_fusion.1
  122.6 5.0 %slice.17 = f32[15,256,512]{2,1,0:T(8,128)} slice(f32[16,256,512]{2,1,0:T(8,128)S(1)} %convolution_bitcast_fusion.1), slice={[0:15], [0:256], [0:512]} | slice | bytes 15728640 | tf_op jit(solution)/shard_map/slice | solution.py:84
  127.6 1.7 convolution_bitcast_fusion
  129.3 3.2 copy-done.1
  132.5 4.6 %slice.18 = f32[15,256,512]{2,1,0:T(8,128)} slice(f32[16,256,512]{2,1,0:T(8,128)S(1)} %convolution_bitcast_fusion), slice={[0:15], [0:256], [0:512]} | slice | bytes 15728640 | tf_op jit(solution)/shard_map/slice | solution.py:85
  137.1 19.0 %multiply_add_fusion.1 = (f32[16,256,512]{2,1,0:T(8,128)}, f32[16,256,512]{2,1,0:T(8,128)}) fusion(f32[16,256,512]{2,1,0:T(8,128)} %copy-done, f32[15,256,512]{2,1,0:T(8,128)} %slice.17, f32[256]{0:T(256)S(1)} %compare_select_fusion.3, f32[16,256,512]{2,1,0:T(8,128)} %copy-done.1, f32[15,256,512]{2,1,0:T(8,128)} %slice.18), kind=kLoop, calls=%fused_computation.25 | loop fusion | flops 8388608 | bytes 49284096 | tf_op jit(solution)/shard_map/add | solution.py:84
  156.1 7.7 %gather_fusion = f32[16,256,512]{2,1,0:T(8,128)} fusion(f32[16,256,512]{2,1,0:T(8,128)} %get-tuple-element.108, s32[1024]{0:T(1024)S(1)} %pad_clamp_fusion), kind=kCustom, calls=%fused_computation.clone | custom fusion | bytes 16777280 | tf_op jit(solution)/shard_map/jit(_take)/gather | solution.py:100
  163.7 9.2 %copy.18 = f32[16,256,512]{1,2,0:T(8,128)} copy(f32[16,256,512]{2,1,0:T(8,128)} %gather_fusion) | data formatting | bytes 16777216 | tf_op jit(solution)/shard_map/jit(_take)/gather | solution.py:100
  173.0 7.7 %gather_fusion.1 = f32[16,256,512]{2,1,0:T(8,128)} fusion(f32[16,256,512]{2,1,0:T(8,128)} %get-tuple-element.109, s32[1024]{0:T(1024)S(1)} %pad_clamp_fusion), kind=kCustom, calls=%fused_computation.1.clone | custom fusion | bytes 16777280 | tf_op jit(solution)/shard_map/jit(_take)/gather | solution.py:101
  180.6 9.3 %copy.20 = f32[16,256,512]{1,2,0:T(8,128)} copy(f32[16,256,512]{2,1,0:T(8,128)} %gather_fusion.1) | data formatting | bytes 16777216 | tf_op jit(solution)/shard_map/jit(_take)/gather | solution.py:101
  189.9 3.5 fusion.57
  193.4 10.9 %fusion.6 = (bf16[256,512]{0,1:T(8,128)(2,1)S(1)}, bf16[256,512]{0,1:T(8,128)(2,1)S(1)}, f32[16,512,256]{2,1,0:T(8,128)}) fusion(f32[16,512,256]{2,1,0:T(8,128)S(1)} %fusion.57, f32[16,256,512]{1,2,0:T(8,128)} %copy.20, f32[16,256,512]{1,2,0:T(8,128)} %copy.18, f32[16]{0:T(128)S(1)} %get-tuple-element.112, pred[16]{0:T(512)(128)(4,1)S(1)} %get-tuple-element.111, ...), kind=kOutput, calls=%fused_computation.14 | convolution fusion | flops 562266112 | bytes 36175952 | tf_op jit(solution)/shard_map/qk,rkb->rqb/dot_general | solution.py:39
  204.3 9.5 %fusion.11 = f32[16,512,256]{2,1,0:T(8,128)} fusion(f32[16,512,256]{2,1,0:T(8,128)} %get-tuple-element.110, f32[16,512,256]{2,1,0:T(8,128)S(1)} %fusion.57, f32[256,512]{0,1:T(8,128)S(1)} %convolution_bitcast_fusion.2, f32[256,512]{0,1:T(8,128)S(1)} %convolution_bitcast_fusion.3, s32[256]{0:T(256)S(1)} %and_select_fusion), kind=kOutput, calls=%fused_computation.26 | convolution fusion | flops 1083113472 | bytes 26215424 | tf_op jit(solution)/shard_map/an,hny->hay/dot_general | solution.py:108
  213.7 11.8 %multiply_bitcast_fusion = f32[16,256,512]{1,2,0:T(8,128)} fusion(f32[16,512,256]{2,1,0:T(8,128)} %fusion.11, f32[16]{0:T(128)S(1)} %broadcast_select_fusion, f32[16,512,256]{2,1,0:T(8,128)} %get-tuple-element.110, f32[16,512,256]{2,1,0:T(8,128)S(1)} %fusion.57, f32[256,512]{0,1:T(8,128)S(1)} %convolution_bitcast_fusion.2, ...), kind=kOutput, calls=%fused_computation.23 | convolution fusion | flops 1087307776 | bytes 34604096 | tf_op jit(solution)/shard_map/an,hny->hay/dot_general | solution.py:106
  225.5 2.6 broadcast_in_dim.30
  228.1 71.4 %while.13 = (s32[]{:T(128)}, f32[2176,512]{1,0:T(8,128)}, s32[16]{0:T(128)S(1)}, f32[16,256,512]{1,2,0:T(8,128)}, s32[]{:T(128)}, /*index=5*/s32[1]{0:T(128)}, s32[]{:T(128)}, s32[]{:T(128)}) while((s32[]{:T(128)}, f32[2176,512]{1,0:T(8,128)}, s32[16]{0:T(128)S(1)}, f32[16,256,512]{1,2,0:T(8,128)}, s32[]{:T(128)}, /*index=5*/s32[1]{0:T(128)}, ...), condition=%wide.region_3.5_spmd, body=%wide.region_2.4_spmd.sunk | while | flops 131078 | bytes 3670167 | solution.py:118
  229.4 1.1 constant_dynamic-slice_fusion.2
  230.7 1.9 fusion.115
  233.8 1.1 constant_dynamic-slice_fusion.2
  235.1 1.9 fusion.115
  238.3 1.1 constant_dynamic-slice_fusion.2
  239.6 1.9 fusion.115
  241.5 0.6 dynamic_slice.28
  242.8 1.1 constant_dynamic-slice_fusion.2
  244.1 1.9 fusion.115
  247.2 1.1 constant_dynamic-slice_fusion.2
  248.5 1.9 fusion.115
  251.7 1.1 constant_dynamic-slice_fusion.2
  253.0 1.9 fusion.115
  256.2 1.1 constant_dynamic-slice_fusion.2
  257.4 1.9 fusion.115
  259.4 0.6 dynamic_slice.28
  260.6 1.1 constant_dynamic-slice_fusion.2
  261.9 1.9 fusion.115
  265.1 1.1 constant_dynamic-slice_fusion.2
  266.3 1.9 fusion.115
  268.3 0.6 dynamic_slice.28
  269.5 1.1 constant_dynamic-slice_fusion.2
  270.8 1.9 fusion.115
  274.0 1.1 constant_dynamic-slice_fusion.2
  275.3 1.9 fusion.115
  277.2 0.6 dynamic_slice.28
  278.5 1.1 constant_dynamic-slice_fusion.2
  279.7 1.9 fusion.115
  282.9 1.1 constant_dynamic-slice_fusion.2
  284.2 1.9 fusion.115
  287.4 1.1 constant_dynamic-slice_fusion.2
  288.7 1.9 fusion.115
  291.9 1.1 constant_dynamic-slice_fusion.2
  293.2 1.9 fusion.115
  296.3 1.1 constant_dynamic-slice_fusion.2
  297.6 1.9 fusion.115
  299.5 3.8 %slice.21 = bf16[2048,512]{1,0:T(8,128)(2,1)} slice(f32[2176,512]{1,0:T(8,128)} %get-tuple-element.83), slice={[128:2176], [0:512]} | slice | bytes 4194304 | tf_op jit(solution)/shard_map/slice | solution.py:130
  303.4 0.7 fusion.32
  304.0 1.4 fusion.24
  305.4 61.7 %reduce-scatter.2.cloned.1.call-done = bf16[128,512]{1,0:T(8,128)(2,1)} async-done(((bf16[2048,512]{1,0:T(8,128)(2,1)}), bf16[128,512]{1,0:T(8,128)(2,1)}) %reduce-scatter.2.cloned.1.call-update) | async-done | bytes 131088 | tf_op jit(solution)/shard_map/reduce_scatter | solution.py:129
  367.2 1.6 convert_multiply_fusion.3
  (52 shorter events, 10.4 us)
Async XLA Ops:
  7.2 104.5 %all-gather.3.cloned.1.call-start = ((), (), s32[]{:S(2)}) async-start(), calls=%async_computation.2 | async-start | bytes 2228224 | tf_op jit(solution)/shard_map/all_gather | solution.py:53
  7.9 111.5 %copy-start.3 = (bf16[128,512]{1,0:T(8,128)(2,1)S(1)}, bf16[128,512]{1,0:T(8,128)(2,1)}, u32[]{:S(2)}) copy-start(bf16[128,512]{1,0:T(8,128)(2,1)} %param.13) | copy-start | bytes 393220
  7.9 111.5 %copy-start.4 = (bf16[128,512]{1,0:T(8,128)(2,1)S(1)}, bf16[128,512]{1,0:T(8,128)(2,1)}, u32[]{:S(2)}) copy-start(bf16[128,512]{1,0:T(8,128)(2,1)} %param.14) | copy-start | bytes 393220
  10.4 110.5 %all-to-all-start = ((bf16[16,128,512]{2,1,0:T(8,128)(2,1)}), bf16[16,128,512]{2,1,0:T(8,128)(2,1)S(1)}, u32[]{:S(2)}, u32[]{:S(2)}) async-start(bf16[16,128,512]{2,1,0:T(8,128)(2,1)} %stack.2), calls=%async_computation | async-start | bytes 4194304 | tf_op jit(solution)/shard_map/all_to_all | solution.py:73
  15.8 174.1 %all-gather.5.cloned.1.call-start = ((), (), s32[]{:S(2)}) async-start(), calls=%async_computation.3 | async-start | bytes 2228224 | tf_op jit(solution)/shard_map/all_gather | solution.py:91
  119.3 247.9 %reduce-scatter.2.cloned.1.call-start = ((), (), s32[]{:S(2)}) async-start(), calls=%async_computation.4 | async-start | bytes 2228224 | tf_op jit(solution)/shard_map/reduce_scatter | solution.py:129
  122.6 6.6 %copy-start = (f32[16,256,512]{2,1,0:T(8,128)}, f32[16,256,512]{2,1,0:T(8,128)S(1)}, u32[]{:S(2)}) copy-start(f32[16,256,512]{2,1,0:T(8,128)S(1)} %convolution_bitcast_fusion.1) | copy-start | bytes 25165828
  129.3 3.2 copy-start.1
  189.9 3.5 copy-start.2
Sparse Core Ops, SparseCore 0:
  10.4 101.2 all-gather.2
  119.4 32.9 all-gather.4
  303.5 63.6 reduce-scatter.1
